TPU v7x, 32 devices: a whole 2x2x4 slice. The times are simulated.
32 devices in a mesh: dp: 8 (over z, y), tensor: 4 (over x, core).
Axes of the slice: x: 2, y: 2, z: 4, core: 2. Of those that a mesh axis runs over, the one named last changes fastest.
Arguments:
- tokens: float32 [4096, 1152], P(('dp', 'tensor')), may hold values from -6 to 6
- timesteps: int32 [16], replicated, may hold values from 0 to 999
- labels: int32 [16], replicated, may hold values from 0 to 1000
- time_weight: float32 [256, 1152], P(None, 'dp'), may hold values from -0.5 to 0.5
- class_table: float32 [1001, 1152], P(None, 'dp'), may hold values from -6 to 6
- mod_weight: bfloat16 [1, 1152, 6912], P(None, 'dp', 'tensor'), may hold values from -0.1875 to 0.1875
- mod_bias: float32 [1, 6912], replicated, may hold values from -3 to 3
- qkv_weight: bfloat16 [1, 3, 1152, 1152], P(None, None, 'dp', 'tensor'), may hold values from -0.1875 to 0.1875
- qv_bias: float32 [1, 2, 1152], replicated, may hold values from -3 to 3
- proj_weight: bfloat16 [1, 1152, 1152], P(None, 'tensor', 'dp'), may hold values from -1.25 to 1.25
- proj_bias: float32 [1, 1152], replicated, may hold values from -3 to 3
- up_weight: bfloat16 [1, 1152, 4608], P(None, 'dp', 'tensor'), may hold values from -0.1875 to 0.1875
- up_bias: float32 [1, 4608], replicated, may hold values from -3 to 3
- down_weight: bfloat16 [1, 4608, 1152], P(None, 'tensor', 'dp'), may hold values from -0.125 to 0.125
- down_bias: float32 [1, 1152], replicated, may hold values from -3 to 3
- grad_output: float32 [4096, 1152], P(('dp', 'tensor')), may hold values from -6 to 6
Outputs:
- output: float32 [4096, 1152], P(('dp', 'tensor'))
- grad_tokens: float32 [4096, 1152], P(('dp', 'tensor'))
- grad_time_weight: float32 [256, 1152], P(None, 'dp')
- grad_class_table: float32 [1001, 1152], P(None, 'dp')
- grad_mod_weight: float32 [1, 1152, 6912], P(None, 'dp', 'tensor')
- grad_mod_bias: float32 [1, 6912], replicated
- grad_qkv_weight: float32 [1, 3, 1152, 1152], P(None, None, 'dp', 'tensor')
- grad_qv_bias: float32 [1, 2, 1152], replicated
- grad_proj_weight: float32 [1, 1152, 1152], P(None, 'tensor', 'dp')
- grad_proj_bias: float32 [1, 1152], replicated
- grad_up_weight: float32 [1, 1152, 4608], P(None, 'dp', 'tensor')
- grad_up_bias: float32 [1, 4608], replicated
- grad_down_weight: float32 [1, 4608, 1152], P(None, 'tensor', 'dp')
- grad_down_bias: float32 [1, 1152], replicated
All inputs are finite; a program needn't handle non-finite values.
Results may differ from a plain program's by a relative error of at most 0.025.
Values may be sent and summed in bfloat16 or wider, within the bound.
A program may use at most 128 MiB of HBM per device.

v0:
```python
import math
import jax
import jax.numpy as jnp
from jax import lax
from jax.sharding import PartitionSpec as P

HEAD_DIM = 72
SEQ = 256
LAYERS = 1
EPSILON = 1e-06
PRECISE = lax.Precision.HIGHEST
GELU_COEFF = math.sqrt(2.0 / math.pi)
CUBIC_COEFF = 0.044715


def time_features(timesteps, width):
    half_width = width // 2
    freq_rates = jnp.exp(
        -math.log(10000.0) * jnp.arange(half_width, dtype=jnp.float32) / half_width
    )
    angles = timesteps.astype(jnp.float32)[:, None] * freq_rates[None, :]
    return jnp.concatenate([jnp.cos(angles), jnp.sin(angles)], axis=1)


def layer_norm(values):
    average = jnp.mean(values, axis=-1, keepdims=True)
    centred = values - average
    inverse = lax.rsqrt(jnp.mean(centred * centred, axis=-1, keepdims=True) + EPSILON)
    return (centred * inverse, inverse)


def norm_back(normed, inverse, grad_normed):
    first = jnp.mean(grad_normed, axis=-1, keepdims=True)
    second = jnp.mean(grad_normed * normed, axis=-1, keepdims=True)
    return inverse * (grad_normed - first - normed * second)


def gelu_value(values):
    return (
        0.5
        * values
        * (1.0 + jnp.tanh(GELU_COEFF * (values + CUBIC_COEFF * values * values * values)))
    )


def gelu_slope(values):
    tangent = jnp.tanh(GELU_COEFF * (values + CUBIC_COEFF * values * values * values))
    return 0.5 * (1.0 + tangent) + 0.5 * values * (1.0 - tangent * tangent) * GELU_COEFF * (
        1.0 + 3.0 * CUBIC_COEFF * values * values
    )


def silu_slope(values):
    logistic = jax.nn.sigmoid(values)
    return logistic * (1.0 + values * (1.0 - logistic))


def split_heads(values, latent_count):
    return values.reshape(latent_count, SEQ, -1, HEAD_DIM)


def local(
    tokens,
    timesteps,
    labels,
    time_weight,
    class_table,
    mod_weight,
    mod_bias,
    qkv_weight,
    qv_bias,
    proj_weight,
    proj_bias,
    up_weight,
    up_bias,
    down_weight,
    down_bias,
    grad_output,
):
    rows_own, model_width = tokens.shape
    tensor_count = lax.axis_size("tensor")
    tensor_place = lax.axis_index("tensor")
    group_rows = rows_own * tensor_count
    latent_count = group_rows // SEQ
    head_cols = qkv_weight.shape[3]
    unit_cols = up_weight.shape[2]
    mod_cols = mod_weight.shape[2]
    head_start = tensor_place * head_cols
    unit_start = tensor_place * unit_cols
    col_start = tensor_place * mod_cols
    score_scale = 1.0 / math.sqrt(HEAD_DIM)
    features = time_features(timesteps, time_weight.shape[0])
    one_hot = (
        labels[:, None] == jnp.arange(class_table.shape[0], dtype=jnp.int32)[None, :]
    ).astype(jnp.float32)
    condition = jnp.dot(features, time_weight, precision=PRECISE) + jnp.dot(
        one_hot, class_table, precision=PRECISE
    )
    cond_act = jax.nn.silu(condition).astype(jnp.bfloat16)
    mod_terms = jnp.stack([jnp.dot(cond_act, mod_weight[0], preferred_element_type=jnp.float32)])
    mod_own = lax.psum_scatter(mod_terms, "dp", scatter_dimension=1, tiled=True)
    mod_own = mod_own + lax.dynamic_slice_in_dim(mod_bias, col_start, mod_cols, 1)[:, None, :]
    modulation = lax.all_gather(mod_own, "tensor", axis=2, tiled=True)
    row_latent = (tensor_place * rows_own + jnp.arange(rows_own, dtype=jnp.int32)) // SEQ
    selector = (row_latent[:, None] == jnp.arange(latent_count, dtype=jnp.int32)[None, :]).astype(
        jnp.float32
    )

    def per_row(values):
        return jnp.dot(selector, values, precision=PRECISE)

    def per_latent(values):
        return jnp.dot(selector.T, values, precision=PRECISE)

    def mod_pieces(current):
        rows_mod = per_row(modulation[current])
        return [
            rows_mod[:, segment * model_width : (segment + 1) * model_width] for segment in range(6)
        ]

    def gather_layer(current):
        return (
            lax.all_gather(qkv_weight[current], "dp", axis=1, tiled=True),
            lax.all_gather(proj_weight[current], "dp", axis=1, tiled=True),
            lax.all_gather(up_weight[current], "dp", axis=0, tiled=True),
            lax.all_gather(down_weight[current], "dp", axis=1, tiled=True),
        )

    def spread_rows(values):
        return lax.all_gather(values, "tensor", axis=0, tiled=True)

    def sum_rows(values):
        return lax.psum_scatter(
            values.astype(jnp.bfloat16), "tensor", scatter_dimension=0, tiled=True
        ).astype(jnp.float32)

    def spread_grads(values):
        return lax.all_gather(values, "tensor", axis=0, tiled=True)

    def sum_grads(values):
        return lax.psum_scatter(
            values.astype(jnp.bfloat16), "tensor", scatter_dimension=0, tiled=True
        ).astype(jnp.float32)

    def attention_scores(queries, key_rows):
        return (
            jnp.einsum(
                "bqhd,bkhd->bhqk",
                split_heads(queries, latent_count),
                split_heads(key_rows, latent_count),
                preferred_element_type=jnp.float32,
            )
            * score_scale
        )

    kept_weights = []
    current_x = tokens
    current = 0
    layer_full = gather_layer(current)
    kept_weights.append(layer_full)
    qkv_full, proj_full, up_full, down_full = layer_full
    shift_attn, scale_attn, gate_attn, shift_mlp, scale_mlp, gate_mlp = mod_pieces(current)
    bias_query = lax.dynamic_slice_in_dim(qv_bias[current, 0], head_start, head_cols, 0)
    bias_value = lax.dynamic_slice_in_dim(qv_bias[current, 1], head_start, head_cols, 0)
    unit_bias = lax.dynamic_slice_in_dim(up_bias[current], unit_start, unit_cols, 0)
    normed_attn, inverse_attn = layer_norm(current_x)
    attn_in = spread_rows((normed_attn * (1.0 + scale_attn) + shift_attn).astype(jnp.bfloat16))
    queries = (
        jnp.dot(attn_in, qkv_full[0], preferred_element_type=jnp.float32) + bias_query
    ).astype(jnp.bfloat16)
    key_rows = jnp.dot(attn_in, qkv_full[1], preferred_element_type=jnp.float32).astype(
        jnp.bfloat16
    )
    value_rows = (
        jnp.dot(attn_in, qkv_full[2], preferred_element_type=jnp.float32) + bias_value
    ).astype(jnp.bfloat16)
    scores = attention_scores(queries, key_rows)
    log_total = jnp.log(jnp.sum(jnp.exp(scores), axis=-1, keepdims=True))
    prob_low = jnp.exp(scores - log_total).astype(jnp.bfloat16)
    attended = (
        jnp.einsum(
            "bhqk,bkhd->bqhd",
            prob_low,
            split_heads(value_rows, latent_count),
            preferred_element_type=jnp.float32,
        )
        .astype(jnp.bfloat16)
        .reshape(group_rows, head_cols)
    )
    attn_out = (
        sum_rows(jnp.dot(attended, proj_full, preferred_element_type=jnp.float32))
        + proj_bias[current]
    )
    middle = current_x + gate_attn * attn_out
    normed_mlp, inverse_mlp = layer_norm(middle)
    mlp_in = spread_rows((normed_mlp * (1.0 + scale_mlp) + shift_mlp).astype(jnp.bfloat16))
    pre_act = jnp.dot(mlp_in, up_full, preferred_element_type=jnp.float32) + unit_bias
    gelu_low = gelu_value(pre_act).astype(jnp.bfloat16)
    mlp_out = (
        sum_rows(jnp.dot(gelu_low, down_full, preferred_element_type=jnp.float32))
        + down_bias[current]
    )
    stored = [
        (
            normed_attn,
            inverse_attn,
            attn_in,
            queries,
            key_rows,
            value_rows,
            log_total,
            attended,
            attn_out,
            normed_mlp,
            inverse_mlp,
            mlp_in,
            pre_act,
            gelu_low,
            mlp_out,
        )
    ]
    current_x = middle + gate_mlp * mlp_out
    grad_x = grad_output
    mod_list = [None] * LAYERS
    qkv_list = [None] * LAYERS
    proj_list = [None] * LAYERS
    up_list = [None] * LAYERS
    down_list = [None] * LAYERS
    qv_bias_list = [None] * LAYERS
    proj_bias_list = [None] * LAYERS
    unit_bias_list = [None] * LAYERS
    down_bias_list = [None] * LAYERS
    for current in reversed(range(LAYERS)):
        (
            normed_attn,
            inverse_attn,
            attn_in,
            queries,
            key_rows,
            value_rows,
            log_total,
            attended,
            attn_out,
            normed_mlp,
            inverse_mlp,
            mlp_in,
            pre_act,
            gelu_low,
            mlp_out,
        ) = stored[current]
        qkv_full, proj_full, up_full, down_full = gather_layer(current)
        shift_attn, scale_attn, gate_attn, shift_mlp, scale_mlp, gate_mlp = mod_pieces(current)
        d_mlp = grad_x * gate_mlp
        d_gate_mlp = per_latent(grad_x * mlp_out)
        down_bias_list[current] = jnp.sum(d_mlp, axis=0)
        d_mlp_all = spread_grads(d_mlp.astype(jnp.bfloat16))
        grad_down = jnp.dot(gelu_low.T, d_mlp_all, preferred_element_type=jnp.float32)
        d_gelu = jnp.dot(d_mlp_all, down_full.T, preferred_element_type=jnp.float32)
        d_pre = d_gelu * gelu_slope(pre_act)
        unit_part = jnp.sum(d_pre, axis=0)
        unit_bias_list[current] = lax.dynamic_update_slice_in_dim(
            jnp.zeros((up_bias.shape[1],), jnp.float32), unit_part, unit_start, 0
        )
        d_pre_low = d_pre.astype(jnp.bfloat16)
        grad_up = jnp.dot(mlp_in.T, d_pre_low, preferred_element_type=jnp.float32)
        d_mlp_in = sum_grads(jnp.dot(d_pre_low, up_full.T, preferred_element_type=jnp.float32))
        d_shift_mlp = per_latent(d_mlp_in)
        d_scale_mlp = per_latent(d_mlp_in * normed_mlp)
        d_middle = grad_x + norm_back(normed_mlp, inverse_mlp, d_mlp_in * (1.0 + scale_mlp))
        d_attn = d_middle * gate_attn
        d_gate_attn = per_latent(d_middle * attn_out)
        proj_bias_list[current] = jnp.sum(d_attn, axis=0)
        d_attn_all = spread_grads(d_attn.astype(jnp.bfloat16))
        grad_proj = jnp.dot(attended.T, d_attn_all, preferred_element_type=jnp.float32)
        d_attended = jnp.dot(d_attn_all, proj_full.T, preferred_element_type=jnp.float32).astype(
            jnp.bfloat16
        )
        scores = attention_scores(queries, key_rows)
        prob_full = jnp.exp(scores - log_total)
        prob_low = prob_full.astype(jnp.bfloat16)
        d_heads = split_heads(d_attended, latent_count)
        grad_value = jnp.einsum(
            "bhqk,bqhd->bkhd", prob_low, d_heads, preferred_element_type=jnp.float32
        ).reshape(group_rows, head_cols)
        d_prob = jnp.einsum(
            "bqhd,bkhd->bhqk",
            d_heads,
            split_heads(value_rows, latent_count),
            preferred_element_type=jnp.float32,
        )
        row_delta = jnp.einsum(
            "bqhd,bqhd->bhq",
            d_heads,
            split_heads(attended, latent_count),
            preferred_element_type=jnp.float32,
        )
        d_scores = prob_full * (d_prob - row_delta[..., None])
        d_score_low = d_scores.astype(jnp.bfloat16)
        grad_query = (
            jnp.einsum(
                "bhqk,bkhd->bqhd",
                d_score_low,
                split_heads(key_rows, latent_count),
                preferred_element_type=jnp.float32,
            ).reshape(group_rows, head_cols)
            * score_scale
        )
        grad_key = (
            jnp.einsum(
                "bhqk,bqhd->bkhd",
                d_score_low,
                split_heads(queries, latent_count),
                preferred_element_type=jnp.float32,
            ).reshape(group_rows, head_cols)
            * score_scale
        )
        qv_part = jnp.stack([jnp.sum(grad_query, axis=0), jnp.sum(grad_value, axis=0)])
        qv_bias_list[current] = lax.dynamic_update_slice_in_dim(
            jnp.zeros((2, model_width), jnp.float32), qv_part, head_start, 1
        )
        query_low = grad_query.astype(jnp.bfloat16)
        key_low = grad_key.astype(jnp.bfloat16)
        value_low = grad_value.astype(jnp.bfloat16)
        grad_qkv = jnp.stack(
            [
                jnp.dot(attn_in.T, query_low, preferred_element_type=jnp.float32),
                jnp.dot(attn_in.T, key_low, preferred_element_type=jnp.float32),
                jnp.dot(attn_in.T, value_low, preferred_element_type=jnp.float32),
            ]
        )
        d_attn_terms = (
            jnp.dot(query_low, qkv_full[0].T, preferred_element_type=jnp.float32)
            + jnp.dot(key_low, qkv_full[1].T, preferred_element_type=jnp.float32)
            + jnp.dot(value_low, qkv_full[2].T, preferred_element_type=jnp.float32)
        )
        d_attn_in = sum_grads(d_attn_terms)
        d_shift_attn = per_latent(d_attn_in)
        d_scale_attn = per_latent(d_attn_in * normed_attn)
        grad_x = d_middle + norm_back(normed_attn, inverse_attn, d_attn_in * (1.0 + scale_attn))
        mod_list[current] = jnp.concatenate(
            [d_shift_attn, d_scale_attn, d_gate_attn, d_shift_mlp, d_scale_mlp, d_gate_mlp], axis=1
        )
        qkv_list[current], proj_list[current], up_list[current], down_list[current] = (
            lax.psum_scatter(
                grad_qkv.astype(jnp.bfloat16), "dp", scatter_dimension=1, tiled=True
            ).astype(jnp.float32),
            lax.psum_scatter(
                grad_proj.astype(jnp.bfloat16), "dp", scatter_dimension=1, tiled=True
            ).astype(jnp.float32),
            lax.psum_scatter(
                grad_up.astype(jnp.bfloat16), "dp", scatter_dimension=0, tiled=True
            ).astype(jnp.float32),
            lax.psum_scatter(
                grad_down.astype(jnp.bfloat16), "dp", scatter_dimension=1, tiled=True
            ).astype(jnp.float32),
        )
    d_mod_part = jnp.stack(mod_list)
    qv_total, proj_total, unit_total, down_total, modb_total = lax.psum(
        (
            jnp.stack(qv_bias_list),
            jnp.stack(proj_bias_list),
            jnp.stack(unit_bias_list),
            jnp.stack(down_bias_list),
            jnp.sum(d_mod_part, axis=1),
        ),
        ("dp", "tensor"),
    )
    d_mod = lax.psum(d_mod_part.astype(jnp.bfloat16), "tensor").astype(jnp.float32)
    d_mod_all = lax.all_gather(
        lax.dynamic_slice_in_dim(d_mod, col_start, mod_cols, 2), "dp", axis=1, tiled=True
    )
    cond_wide = cond_act.astype(jnp.float32)
    grad_mod_weight = jnp.stack([jnp.dot(cond_wide.T, d_mod_all[0], precision=PRECISE)])
    cond_back = jnp.dot(d_mod_all[0], mod_weight[0].astype(jnp.float32).T, precision=PRECISE)
    d_cond_act = lax.psum(cond_back, "tensor")
    d_condition = d_cond_act * silu_slope(condition)
    grad_time_weight = jnp.dot(features.T, d_condition, precision=PRECISE)
    grad_class_table = jnp.dot(one_hot.T, d_condition, precision=PRECISE)
    return (
        current_x,
        grad_x,
        grad_time_weight,
        grad_class_table,
        grad_mod_weight,
        modb_total,
        jnp.stack(qkv_list),
        qv_total,
        jnp.stack(proj_list),
        proj_total,
        jnp.stack(up_list),
        unit_total,
        jnp.stack(down_list),
        down_total,
    )


def solution(mesh):
    in_specs = (
        P(("dp", "tensor"), None),
        P(),
        P(),
        P(None, "dp"),
        P(None, "dp"),
        P(None, "dp", "tensor"),
        P(),
        P(None, None, "dp", "tensor"),
        P(),
        P(None, "tensor", "dp"),
        P(),
        P(None, "dp", "tensor"),
        P(),
        P(None, "tensor", "dp"),
        P(),
        P(("dp", "tensor"), None),
    )
    out_specs = (
        P(("dp", "tensor"), None),
        P(("dp", "tensor"), None),
        P(None, "dp"),
        P(None, "dp"),
        P(None, "dp", "tensor"),
        P(),
        P(None, None, "dp", "tensor"),
        P(),
        P(None, "tensor", "dp"),
        P(),
        P(None, "dp", "tensor"),
        P(),
        P(None, "tensor", "dp"),
        P(),
    )
    return jax.shard_map(local, mesh=mesh, in_specs=in_specs, out_specs=out_specs, check_vma=False)
```

profile of v0, /device:TPU:0, one launch (start us, length us, event | category | flops | bytes accessed | tf_op | source)
XLA Modules:
  0.0 829.4 jit_solution(17721218927461385044)
XLA Ops:
  16.1 69.0 %all-reduce.4.cloned.1.call-done = f32[1,16,1728]{2,1,0:T(8,128)} async-done(((f32[1,16,1728]{2,1,0:T(8,128)}), f32[1,16,1728]{2,1,0:T(8,128)}) %all-reduce.4.cloned.1.call-update) | async-done | bytes 110608
  87.2 23.5 %all_gather.34 = f32[1,2,6912]{1,0,2:T(1,128)S(1)} all-gather(f32[1,2,1728]{1,0,2:T(1,128)S(1)} %copy.63), channel_id=1, replica_groups=mesh['dp'=8,'tensor'=4] {'tensor'}, dimensions={2}, use_global_device_ids=true | all-gather | bytes 69120 | tf_op jit(solution)/shard_map/all_gather | solution.py:103
  116.6 35.3 %all-gather.1 = bf16[1,288,1152]{1,2,0:T(8,128)(2,1)} all-gather(bf16[1,288,144]{1,2,0:T(8,128)(2,1)S(1)} %copy-done.24), channel_id=3, replica_groups=mesh['dp'=8,'tensor'=4] {'dp'}, dimensions={2}, use_global_device_ids=true | all-gather | bytes 746496 | tf_op jit(solution)/shard_map/all_gather | solution.py:124
  151.9 38.0 %all-gather.20.cloned.1.call-done = bf16[1,3,1152,288]{3,2,1,0:T(8,128)(2,1)} async-done(((bf16[1,3,144,288]{3,2,1,0:T(8,128)(2,1)}), bf16[1,3,1152,288]{3,2,1,0:T(8,128)(2,1)}) %all-gather.20.cloned.1.call-update) | async-done | bytes 1990672 | tf_op jit(solution)/shard_map/all_gather | solution.py:123
  205.9 23.6 %reduce-scatter.12.cloned.1.call-done = bf16[128,1152]{1,0:T(8,128)(2,1)} async-done(((bf16[512,1152]{1,0:T(8,128)(2,1)}), bf16[128,1152]{1,0:T(8,128)(2,1)}) %reduce-scatter.12.cloned.1.call-update) | async-done | bytes 294928 | tf_op jit(solution)/shard_map/reduce_scatter | solution.py:133
  236.2 50.3 %all-gather.22.cloned.1.call-done = bf16[1,1152,1152]{2,1,0:T(8,128)(2,1)} async-done(((bf16[1,144,1152]{2,1,0:T(8,128)(2,1)}), bf16[1,1152,1152]{2,1,0:T(8,128)(2,1)}) %all-gather.22.cloned.1.call-update) | async-done | bytes 2654224 | tf_op jit(solution)/shard_map/all_gather | solution.py:125
  286.5 18.0 %all-gather.14.cloned.1.call-done = bf16[512,1152]{1,0:T(8,128)(2,1)} async-done(((bf16[128,1152]{1,0:T(8,128)(2,1)}), bf16[512,1152]{1,0:T(8,128)(2,1)}) %all-gather.14.cloned.1.call-update) | async-done | bytes 1179664 | tf_op jit(solution)/shard_map/all_gather | solution.py:130
  309.9 51.8 %all-gather.24.cloned.1.call-done = bf16[1,1152,1152]{1,2,0:T(8,128)(2,1)} async-done(((bf16[1,1152,144]{1,2,0:T(8,128)(2,1)}), bf16[1,1152,1152]{1,2,0:T(8,128)(2,1)}) %all-gather.24.cloned.1.call-update) | async-done | bytes 2654224 | tf_op jit(solution)/shard_map/all_gather | solution.py:126
  361.7 18.2 %all-gather.16.cloned.1.call-done = bf16[512,1152]{1,0:T(8,128)(2,1)} async-done(((bf16[128,1152]{1,0:T(8,128)(2,1)}), bf16[512,1152]{1,0:T(8,128)(2,1)}) %all-gather.16.cloned.1.call-update) | async-done | bytes 1179664 | tf_op jit(solution)/shard_map/all_gather | solution.py:138
  379.9 6.0 fusion.104
  389.9 5.7 convolution_convert_fusion.3
  396.3 19.3 %reduce-scatter.16.cloned.1.call-done = bf16[128,1152]{1,0:T(8,128)(2,1)} async-done(((bf16[512,1152]{1,0:T(8,128)(2,1)}), bf16[128,1152]{1,0:T(8,128)(2,1)}) %reduce-scatter.16.cloned.1.call-update) | async-done | bytes 294928 | tf_op jit(solution)/shard_map/reduce_scatter | solution.py:141
  418.1 25.6 %reduce-scatter.14.cloned.1.call-done = bf16[128,1152]{1,0:T(8,128)(2,1)} async-done(((bf16[512,1152]{1,0:T(8,128)(2,1)}), bf16[128,1152]{1,0:T(8,128)(2,1)}) %reduce-scatter.14.cloned.1.call-update) | async-done | bytes 294928 | tf_op jit(solution)/shard_map/reduce_scatter | solution.py:133
  451.5 5.4 convolution_convert_fusion
  498.4 7.2 copy.97
  505.6 7.5 reshape.264
  513.6 25.8 %reduce-scatter.22.cloned.1.call-done = bf16[144,1152]{1,0:T(8,128)(2,1)} async-done(((bf16[1152,1152]{1,0:T(8,128)(2,1)}), bf16[144,1152]{1,0:T(8,128)(2,1)}) %reduce-scatter.22.cloned.1.call-update) | async-done | bytes 331792 | tf_op jit(solution)/shard_map/reduce_scatter | solution.py:350
  541.2 72.6 %reduce-scatter.24.cloned.1.call-done = bf16[1152,144]{0,1:T(8,128)(2,1)} async-done(((bf16[1152,1152]{0,1:T(8,128)(2,1)}), bf16[1152,144]{0,1:T(8,128)(2,1)}) %reduce-scatter.24.cloned.1.call-update) | async-done | bytes 331792 | tf_op jit(solution)/shard_map/reduce_scatter | solution.py:353
  615.7 63.0 %reduce-scatter.20.cloned.1.call-done = bf16[288,144]{0,1:T(8,128)(2,1)} async-done(((bf16[288,1152]{0,1:T(8,128)(2,1)}), bf16[288,144]{0,1:T(8,128)(2,1)}) %reduce-scatter.20.cloned.1.call-update) | async-done | bytes 82960 | tf_op jit(solution)/shard_map/reduce_scatter | solution.py:347
  680.3 25.2 %reduce-scatter.18.cloned.1.call-done = bf16[128,1152]{1,0:T(8,128)(2,1)} async-done(((bf16[512,1152]{1,0:T(8,128)(2,1)}), bf16[128,1152]{1,0:T(8,128)(2,1)}) %reduce-scatter.18.cloned.1.call-update) | async-done | bytes 294928 | tf_op jit(solution)/shard_map/reduce_scatter | solution.py:141
  719.6 10.7 %psum.49 = bf16[1,2,6912]{2,1,0:T(2,128)(2,1)S(1)} all-reduce(bf16[1,2,6912]{2,1,0:T(2,128)(2,1)S(1)} %copy-done.35), channel_id=1, replica_groups=mesh['dp'=8,'tensor'=4] {'tensor'}, use_global_device_ids=true, to_apply=%region_14.15 | all-reduce | flops 13824 | bytes 55296 | tf_op jit(solution)/shard_map/psum | solution.py:368
  730.4 31.0 %all_gather.43 = f32[1,16,1728]{2,0,1:T(1,128)S(1)} all-gather(f32[1,2,1728]{2,0,1:T(1,128)S(1)} %copy.81), channel_id=1, replica_groups=mesh['dp'=8,'tensor'=4] {'dp'}, dimensions={1}, use_global_device_ids=true | all-gather | bytes 124416 | tf_op jit(solution)/shard_map/all_gather | solution.py:369
  761.9 11.0 %psum.50 = f32[16,144]{1,0:T(8,128)S(1)} all-reduce(f32[16,144]{1,0:T(8,128)S(1)} %fusion.39), channel_id=1, replica_groups=mesh['dp'=8,'tensor'=4] {'tensor'}, use_global_device_ids=true, to_apply=%region_15.16 | all-reduce | flops 2304 | bytes 18432 | tf_op jit(solution)/shard_map/psum | solution.py:375
  772.9 40.4 %all-reduce.1 = (f32[1,6912]{1,0:T(1,128)}, f32[1,2,1152]{2,1,0:T(2,128)}, f32[1,1152]{1,0:T(1,128)}, f32[1,4608]{1,0:T(1,128)}, f32[1,1152]{1,0:T(1,128)}) all-reduce(f32[1,6912]{1,0:T(1,128)S(1)} %reduce_sum.147, f32[1,2,1152]{2,1,0:T(2,128)S(1)} %copy-done.33, ...), channel_id=1, replica_groups=mesh['dp'=8,'tensor'=4] {'dp','tensor'}, use_global_device_ids=true, to_apply=%region_17.18 | all-reduce | flops 16128 | bytes 129024 | tf_op jit(solution)/shard_map/psum | solution.py:358
  (250 shorter events, 129.4 us)
Async XLA Ops:
  7.2 77.9 %all-reduce.4.cloned.1.call-start = ((), (), s32[]{:S(2)}) async-start(), calls=%async_computation.23 | async-start | bytes 229376
  12.6 139.3 %all-gather.12.cloned.1.call-start = ((), (), s32[]{:S(2)}) async-start(), calls=%async_computation.8 | async-start | bytes 1474560 | tf_op jit(solution)/shard_map/all_gather | solution.py:130
  13.8 99.2 %copy-start.37 = (f32[128]{0:T(128)}, f32[128]{0:T(128)S(1)}, u32[]{:S(2)}) copy-start(f32[128]{0:T(128)S(1)} %broadcast_multiply_fusion.5) | copy-start | bytes 1540
  14.0 99.0 %copy-start.41 = (f32[128]{0:T(128)}, f32[128]{0:T(128)S(1)}, u32[]{:S(2)}) copy-start(f32[128]{0:T(128)S(1)} %add_rsqrt_fusion.1) | copy-start | bytes 1540
  115.7 74.2 %all-gather.20.cloned.1.call-start = ((), (), s32[]{:S(2)}) async-start(), calls=%async_computation.19 | async-start | bytes 2985984 | tf_op jit(solution)/shard_map/all_gather | solution.py:123
  116.5 113.0 %reduce-scatter.12.cloned.1.call-start = ((), (), s32[]{:S(2)}) async-start(), calls=%async_computation.9 | async-start | bytes 1474560 | tf_op jit(solution)/shard_map/reduce_scatter | solution.py:133
  205.2 81.3 %all-gather.22.cloned.1.call-start = ((), (), s32[]{:S(2)}) async-start(), calls=%async_computation.20 | async-start | bytes 2985984 | tf_op jit(solution)/shard_map/all_gather | solution.py:125
  205.8 98.8 %all-gather.14.cloned.1.call-start = ((), (), s32[]{:S(2)}) async-start(), calls=%async_computation.10 | async-start | bytes 1474560 | tf_op jit(solution)/shard_map/all_gather | solution.py:130
  230.8 184.8 %copy-start.39 = (f32[128]{0:T(128)}, f32[128]{0:T(128)S(1)}, u32[]{:S(2)}) copy-start(f32[128]{0:T(128)S(1)} %broadcast_multiply_fusion.4) | copy-start | bytes 1540
  231.0 184.6 %copy-start.43 = (f32[128]{0:T(128)}, f32[128]{0:T(128)S(1)}, u32[]{:S(2)}) copy-start(f32[128]{0:T(128)S(1)} %add_rsqrt_fusion) | copy-start | bytes 1540
  233.5 128.2 %all-gather.24.cloned.1.call-start = ((), (), s32[]{:S(2)}) async-start(), calls=%async_computation.21 | async-start | bytes 2985984 | tf_op jit(solution)/shard_map/all_gather | solution.py:126
  234.3 145.6 %all-gather.16.cloned.1.call-start = ((), (), s32[]{:S(2)}) async-start(), calls=%async_computation.12 | async-start | bytes 1474560 | tf_op jit(solution)/shard_map/all_gather | solution.py:138
  235.0 180.6 %reduce-scatter.16.cloned.1.call-start = ((), (), s32[]{:S(2)}) async-start(), calls=%async_computation.13 | async-start | bytes 1474560 | tf_op jit(solution)/shard_map/reduce_scatter | solution.py:141
  389.9 53.8 %reduce-scatter.14.cloned.1.call-start = ((), (), s32[]{:S(2)}) async-start(), calls=%async_computation.11 | async-start | bytes 1474560 | tf_op jit(solution)/shard_map/reduce_scatter | solution.py:133
  395.7 68.4 %all-gather.18.cloned.1.call-start = ((), (), s32[]{:S(2)}) async-start(), calls=%async_computation.14 | async-start | bytes 1474560 | tf_op jit(solution)/shard_map/all_gather | solution.py:138
  446.5 92.9 %reduce-scatter.22.cloned.1.call-start = ((), (), s32[]{:S(2)}) async-start(), calls=%async_computation.17 | async-start | bytes 2985984 | tf_op jit(solution)/shard_map/reduce_scatter | solution.py:350
  451.4 162.4 %reduce-scatter.24.cloned.1.call-start = ((), (), s32[]{:S(2)}) async-start(), calls=%async_computation.18 | async-start | bytes 2985984 | tf_op jit(solution)/shard_map/reduce_scatter | solution.py:353
  457.0 221.7 %reduce-scatter.20.cloned.1.call-start = ((), (), s32[]{:S(2)}) async-start(), calls=%async_computation.16 | async-start | bytes 995328 | tf_op jit(solution)/shard_map/reduce_scatter | solution.py:347
  477.8 227.7 %reduce-scatter.18.cloned.1.call-start = ((), (), s32[]{:S(2)}) async-start(), calls=%async_computation.15 | async-start | bytes 1474560 | tf_op jit(solution)/shard_map/reduce_scatter | solution.py:141
  491.2 328.2 %reduce-scatter.26.cloned.1.call-start = ((), (), s32[]{:S(2)}) async-start(), calls=%async_computation.22 | async-start | bytes 2322432
  513.3 196.2 %copy-start.17 = (bf16[128,1152]{1,0:T(8,128)(2,1)S(1)}, bf16[128,1152]{1,0:T(8,128)(2,1)}, u32[]{:S(2)}) copy-start(bf16[128,1152]{1,0:T(8,128)(2,1)} %reduce-scatter.12.cloned.1.call-done) | copy-start | bytes 884740
  513.3 197.9 %copy-start.10 = (bf16[128,1152]{1,0:T(8,128)(2,1)S(1)}, bf16[128,1152]{1,0:T(8,128)(2,1)}, u32[]{:S(2)}) copy-start(bf16[128,1152]{1,0:T(8,128)(2,1)} %reduce-scatter.16.cloned.1.call-done) | copy-start | bytes 884740
  513.5 166.7 %copy-start.32 = (f32[1,2,1152]{2,1,0:T(2,128)}, f32[1,2,1152]{2,1,0:T(2,128)S(1)}, u32[]{:S(2)}) copy-start(f32[1,2,1152]{2,1,0:T(2,128)S(1)} %dynamic_update_slice.8) | copy-start | bytes 27652
  541.2 173.3 %copy-start.18 = (bf16[128,1152]{1,0:T(8,128)(2,1)S(1)}, bf16[128,1152]{1,0:T(8,128)(2,1)}, u32[]{:S(2)}) copy-start(bf16[128,1152]{1,0:T(8,128)(2,1)} %reduce-scatter.14.cloned.1.call-done) | copy-start | bytes 884740
  (44 other events, 1106.1 us)
Sparse Core Ops, SparseCore 0:
  12.7 72.4 all-reduce.3
  115.8 16.3 all-gather.11
  134.5 55.3 all-gather.19
  205.3 24.1 reduce-scatter.11
  231.5 54.9 all-gather.21
  288.5 15.9 all-gather.13
  306.7 54.9 all-gather.23
  363.9 15.9 all-gather.15
  390.0 25.6 reduce-scatter.15
  418.1 25.6 reduce-scatter.13
  446.6 17.4 all-gather.17
  467.6 71.7 reduce-scatter.21
  543.0 70.7 reduce-scatter.23
  617.6 60.9 reduce-scatter.19
  681.1 24.3 reduce-scatter.17
  708.9 68.0 reduce-scatter.25
where the time goes:
time: 838 us; the launch traced here: 829 us
  waiting for transfers between devices  506 us (60%)
  blocking collectives  152 us (18%)
  matrix products  82.3 us (10%)
  local copies, waits for them, and re-layouts  39.9 us (5%)
  other arithmetic  32.1 us (4%)
  between operations  15.7 us (2%)
    reduce_scatter x1, waiting for transfers between devices, local(): lax.psum_scatter(grad_down.astype(jnp.bfloat16), 'dp', scatter_dimension=...  72.6 us
    unnamed x18, waiting for transfers between devices  71.8 us
    reduce_scatter x1, waiting for transfers between devices, local(): lax.psum_scatter(grad_proj.astype(jnp.bfloat16), 'dp', scatter_dimension=...  63 us
    all_gather x1, waiting for transfers between devices, gather_layer(): lax.all_gather(down_weight[current], 'dp', axis=1, tiled=True)  51.8 us
    all_gather x1, waiting for transfers between devices, gather_layer(): lax.all_gather(up_weight[current], 'dp', axis=0, tiled=True)  50.3 us
    reduce_scatter x2, waiting for transfers between devices, sum_rows(): lax.psum_scatter(values.astype(jnp.bfloat16), 'tensor', scatter_dimension...  49.2 us
    reduce_scatter x2, waiting for transfers between devices, sum_grads(): lax.psum_scatter(values.astype(jnp.bfloat16), 'tensor', scatter_dimension...  44.5 us
    psum x1, blocking collectives, local(): lax.psum((jnp.stack(qv_bias_list), jnp.stack(proj_bias_list), jnp.stack(u...  40.4 us
  transfers between devices with their start and end apart: 16, of which 14 were waited for; matrix products, arithmetic and copies ran while one was open for 13% of the time, Pallas kernels for 0%

commit v1 on v0

--- a/solution.py
+++ b/solution.py
@@ -1,3 +1,4 @@
+import functools
 import math
 import jax
 import jax.numpy as jnp
@@ -11,6 +12,22 @@
 PRECISE = lax.Precision.HIGHEST
 GELU_COEFF = math.sqrt(2.0 / math.pi)
 CUBIC_COEFF = 0.044715
+
+
+def guide_meshes_on(sample, which_axis):
+    long_array = jnp.concatenate(
+        jax.lax.all_to_all(
+            jnp.stack([sample] * jax.lax.axis_size(which_axis), axis=0),
+            axis_name=which_axis,
+            split_axis=0,
+            concat_axis=0,
+        ),
+        1,
+    )
+    return long_array
+
+
+treat_ladders_on = functools.partial(guide_meshes_on, which_axis="dp")
 
 
 def time_features(timesteps, width):
@@ -123,7 +140,7 @@
             lax.all_gather(qkv_weight[current], "dp", axis=1, tiled=True),
             lax.all_gather(proj_weight[current], "dp", axis=1, tiled=True),
             lax.all_gather(up_weight[current], "dp", axis=0, tiled=True),
-            lax.all_gather(down_weight[current], "dp", axis=1, tiled=True),
+            treat_ladders_on(down_weight[current]),
         )
 
     def spread_rows(values):

time: 838 us -> 799 us (0.953)
  waiting for transfers between devices: 506 us -> 461 us
    all_gather x1 -> x0, waiting for transfers between devices: 51.8 us -> none  [gather_layer(): lax.all_gather(down_weight[current], 'dp', axis=1, tiled=True)]
    all_gather x1, waiting for transfers between devices: 50.3 us -> 68 us  [gather_layer(): lax.all_gather(up_weight[current], 'dp', axis=0, tiled=True)]
    unnamed x120 -> x122, local copies, waits for them, and re-layouts: 26.8 us -> 26.1 us
    unnamed x18 -> x17, waiting for transfers between devices: 71.8 us -> 71.1 us
  transfers between devices with their start and end apart: 16 -> 16, of which waited for: 14 -> 13; matrix products, arithmetic and copies ran while one was open for 13% -> 14% of each run, Pallas kernels for 0% -> 0%
where the time goes in v1:
time: 799 us; the launch traced here: 790 us
  waiting for transfers between devices  461 us (58%)
  blocking collectives  152 us (19%)
  matrix products  82.3 us (10%)
  local copies, waits for them, and re-layouts  40.9 us (5%)
  other arithmetic  32.2 us (4%)
  between operations  15.7 us (2%)
    reduce_scatter x1, waiting for transfers between devices, local(): lax.psum_scatter(grad_down.astype(jnp.bfloat16), 'dp', scatter_dimension=...  72.4 us
    unnamed x17, waiting for transfers between devices  71.1 us
    all_gather x1, waiting for transfers between devices, gather_layer(): lax.all_gather(up_weight[current], 'dp', axis=0, tiled=True)  68 us
    reduce_scatter x1, waiting for transfers between devices, local(): lax.psum_scatter(grad_proj.astype(jnp.bfloat16), 'dp', scatter_dimension=...  63.3 us
    reduce_scatter x2, waiting for transfers between devices, sum_grads(): lax.psum_scatter(values.astype(jnp.bfloat16), 'tensor', scatter_dimension...  44.5 us
    reduce_scatter x2, waiting for transfers between devices, sum_rows(): lax.psum_scatter(values.astype(jnp.bfloat16), 'tensor', scatter_dimension...  43.1 us
    psum x1, blocking collectives, local(): lax.psum((jnp.stack(qv_bias_list), jnp.stack(proj_bias_list), jnp.stack(u...  40.2 us
    all_gather x1, waiting for transfers between devices, gather_layer(): lax.all_gather(qkv_weight[current], 'dp', axis=1, tiled=True)  38 us
  transfers between devices with their start and end apart: 16, of which 13 were waited for; matrix products, arithmetic and copies ran while one was open for 14% of the time, Pallas kernels for 0%

profile of v1, /device:TPU:0, one launch (start us, length us, event | category | flops | bytes accessed | tf_op | source)
XLA Modules:
  0.0 790.3 jit_solution(16258642754266853082)
XLA Ops:
  16.1 69.0 %all-reduce.4.cloned.1.call-done = f32[1,16,1728]{2,1,0:T(8,128)} async-done(((f32[1,16,1728]{2,1,0:T(8,128)}), f32[1,16,1728]{2,1,0:T(8,128)}) %all-reduce.4.cloned.1.call-update) | async-done | bytes 110608
  87.2 23.5 %all_gather.30 = f32[1,2,6912]{1,0,2:T(1,128)S(1)} all-gather(f32[1,2,1728]{1,0,2:T(1,128)S(1)} %copy.64), channel_id=1, replica_groups=mesh['dp'=8,'tensor'=4] {'tensor'}, dimensions={2}, use_global_device_ids=true | all-gather | bytes 69120 | tf_op jit(solution)/shard_map/all_gather | solution.py:120
  116.6 35.3 %all-gather.1 = bf16[1,288,1152]{1,2,0:T(8,128)(2,1)} all-gather(bf16[1,288,144]{1,2,0:T(8,128)(2,1)S(1)} %copy-done.25), channel_id=3, replica_groups=mesh['dp'=8,'tensor'=4] {'dp'}, dimensions={2}, use_global_device_ids=true | all-gather | bytes 746496 | tf_op jit(solution)/shard_map/all_gather | solution.py:141
  151.9 38.0 %all-gather.18.cloned.1.call-done = bf16[1,3,1152,288]{3,2,1,0:T(8,128)(2,1)} async-done(((bf16[1,3,144,288]{3,2,1,0:T(8,128)(2,1)}), bf16[1,3,1152,288]{3,2,1,0:T(8,128)(2,1)}) %all-gather.18.cloned.1.call-update) | async-done | bytes 1990672 | tf_op jit(solution)/shard_map/all_gather | solution.py:140
  211.6 17.3 %reduce-scatter.12.cloned.1.call-done = bf16[128,1152]{1,0:T(8,128)(2,1)} async-done(((bf16[512,1152]{1,0:T(8,128)(2,1)}), bf16[128,1152]{1,0:T(8,128)(2,1)}) %reduce-scatter.12.cloned.1.call-update) | async-done | bytes 294928 | tf_op jit(solution)/shard_map/reduce_scatter | solution.py:150
  234.9 68.0 %all-gather.20.cloned.1.call-done = bf16[1,1152,1152]{2,1,0:T(8,128)(2,1)} async-done(((bf16[1,144,1152]{2,1,0:T(8,128)(2,1)}), bf16[1,1152,1152]{2,1,0:T(8,128)(2,1)}) %all-gather.20.cloned.1.call-update) | async-done | bytes 2654224 | tf_op jit(solution)/shard_map/all_gather | solution.py:142
  302.9 18.3 %all-gather.12.cloned.1.call-done = bf16[512,1152]{1,0:T(8,128)(2,1)} async-done(((bf16[128,1152]{1,0:T(8,128)(2,1)}), bf16[512,1152]{1,0:T(8,128)(2,1)}) %all-gather.12.cloned.1.call-update) | async-done | bytes 1179664 | tf_op jit(solution)/shard_map/all_gather | solution.py:147
  321.2 5.4 convolution_add_fusion.2
  326.6 14.2 %all-gather.14.cloned.1.call-done = bf16[512,1152]{1,0:T(8,128)(2,1)} async-done(((bf16[128,1152]{1,0:T(8,128)(2,1)}), bf16[512,1152]{1,0:T(8,128)(2,1)}) %all-gather.14.cloned.1.call-update) | async-done | bytes 1179664 | tf_op jit(solution)/shard_map/all_gather | solution.py:155
  340.8 6.0 fusion.102
  350.9 5.7 convolution_convert_fusion.3
  357.3 19.3 %reduce-scatter.16.cloned.1.call-done = bf16[128,1152]{1,0:T(8,128)(2,1)} async-done(((bf16[512,1152]{1,0:T(8,128)(2,1)}), bf16[128,1152]{1,0:T(8,128)(2,1)}) %reduce-scatter.16.cloned.1.call-update) | async-done | bytes 294928 | tf_op jit(solution)/shard_map/reduce_scatter | solution.py:158
  379.0 25.8 %reduce-scatter.14.cloned.1.call-done = bf16[128,1152]{1,0:T(8,128)(2,1)} async-done(((bf16[512,1152]{1,0:T(8,128)(2,1)}), bf16[128,1152]{1,0:T(8,128)(2,1)}) %reduce-scatter.14.cloned.1.call-update) | async-done | bytes 294928 | tf_op jit(solution)/shard_map/reduce_scatter | solution.py:150
  412.6 5.4 convolution_convert_fusion
  459.5 7.2 copy.98
  466.7 7.5 reshape.274
  474.6 25.4 %reduce-scatter.22.cloned.1.call-done = bf16[144,1152]{1,0:T(8,128)(2,1)} async-done(((bf16[1152,1152]{1,0:T(8,128)(2,1)}), bf16[144,1152]{1,0:T(8,128)(2,1)}) %reduce-scatter.22.cloned.1.call-update) | async-done | bytes 331792 | tf_op jit(solution)/shard_map/reduce_scatter | solution.py:367
  501.9 72.4 %reduce-scatter.24.cloned.1.call-done = bf16[1152,144]{0,1:T(8,128)(2,1)} async-done(((bf16[1152,1152]{0,1:T(8,128)(2,1)}), bf16[1152,144]{0,1:T(8,128)(2,1)}) %reduce-scatter.24.cloned.1.call-update) | async-done | bytes 331792 | tf_op jit(solution)/shard_map/reduce_scatter | solution.py:370
  576.2 63.3 %reduce-scatter.20.cloned.1.call-done = bf16[288,144]{0,1:T(8,128)(2,1)} async-done(((bf16[288,1152]{0,1:T(8,128)(2,1)}), bf16[288,144]{0,1:T(8,128)(2,1)}) %reduce-scatter.20.cloned.1.call-update) | async-done | bytes 82960 | tf_op jit(solution)/shard_map/reduce_scatter | solution.py:364
  641.2 25.2 %reduce-scatter.18.cloned.1.call-done = bf16[128,1152]{1,0:T(8,128)(2,1)} async-done(((bf16[512,1152]{1,0:T(8,128)(2,1)}), bf16[128,1152]{1,0:T(8,128)(2,1)}) %reduce-scatter.18.cloned.1.call-update) | async-done | bytes 294928 | tf_op jit(solution)/shard_map/reduce_scatter | solution.py:158
  680.5 10.7 %psum.49 = bf16[1,2,6912]{2,1,0:T(2,128)(2,1)S(1)} all-reduce(bf16[1,2,6912]{2,1,0:T(2,128)(2,1)S(1)} %copy-done.36), channel_id=1, replica_groups=mesh['dp'=8,'tensor'=4] {'tensor'}, use_global_device_ids=true, to_apply=%region_14.15 | all-reduce | flops 13824 | bytes 55296 | tf_op jit(solution)/shard_map/psum | solution.py:385
  691.2 31.3 %all_gather.38 = f32[1,16,1728]{2,0,1:T(1,128)S(1)} all-gather(f32[1,2,1728]{2,0,1:T(1,128)S(1)} %copy.82), channel_id=1, replica_groups=mesh['dp'=8,'tensor'=4] {'dp'}, dimensions={1}, use_global_device_ids=true | all-gather | bytes 124416 | tf_op jit(solution)/shard_map/all_gather | solution.py:386
  723.0 11.0 %psum.50 = f32[16,144]{1,0:T(8,128)S(1)} all-reduce(f32[16,144]{1,0:T(8,128)S(1)} %fusion.37), channel_id=1, replica_groups=mesh['dp'=8,'tensor'=4] {'tensor'}, use_global_device_ids=true, to_apply=%region_15.16 | all-reduce | flops 2304 | bytes 18432 | tf_op jit(solution)/shard_map/psum | solution.py:392
  734.0 40.2 %all-reduce.1 = (f32[1,6912]{1,0:T(1,128)}, f32[1,2,1152]{2,1,0:T(2,128)}, f32[1,1152]{1,0:T(1,128)}, f32[1,4608]{1,0:T(1,128)}, f32[1,1152]{1,0:T(1,128)}) all-reduce(f32[1,6912]{1,0:T(1,128)S(1)} %reduce_sum.147, f32[1,2,1152]{2,1,0:T(2,128)S(1)} %copy-done.34, ...), channel_id=1, replica_groups=mesh['dp'=8,'tensor'=4] {'dp','tensor'}, use_global_device_ids=true, to_apply=%region_17.18 | all-reduce | flops 16128 | bytes 129024 | tf_op jit(solution)/shard_map/psum | solution.py:375
  (252 shorter events, 129.0 us)
Async XLA Ops:
  7.2 77.9 %all-reduce.4.cloned.1.call-start = ((), (), s32[]{:S(2)}) async-start(), calls=%async_computation.23 | async-start | bytes 229376
  12.6 139.3 %all-gather.10.cloned.1.call-start = ((), (), s32[]{:S(2)}) async-start(), calls=%async_computation.9 | async-start | bytes 1474560 | tf_op jit(solution)/shard_map/all_gather | solution.py:147
  13.8 99.2 %copy-start.38 = (f32[128]{0:T(128)}, f32[128]{0:T(128)S(1)}, u32[]{:S(2)}) copy-start(f32[128]{0:T(128)S(1)} %broadcast_multiply_fusion.5) | copy-start | bytes 1540
  14.0 99.0 %copy-start.42 = (f32[128]{0:T(128)}, f32[128]{0:T(128)S(1)}, u32[]{:S(2)}) copy-start(f32[128]{0:T(128)S(1)} %add_rsqrt_fusion.1) | copy-start | bytes 1540
  115.7 74.2 %all-gather.18.cloned.1.call-start = ((), (), s32[]{:S(2)}) async-start(), calls=%async_computation.20 | async-start | bytes 2985984 | tf_op jit(solution)/shard_map/all_gather | solution.py:140
  116.5 112.4 %reduce-scatter.12.cloned.1.call-start = ((), (), s32[]{:S(2)}) async-start(), calls=%async_computation.10 | async-start | bytes 1474560 | tf_op jit(solution)/shard_map/reduce_scatter | solution.py:150
  204.6 98.4 %all-gather.20.cloned.1.call-start = ((), (), s32[]{:S(2)}) async-start(), calls=%async_computation.21 | async-start | bytes 2985984 | tf_op jit(solution)/shard_map/all_gather | solution.py:142
  206.9 119.6 %all-to-all-start = ((bf16[8,1152,144]{1,2,0:T(8,128)(2,1)}), bf16[8,1152,144]{1,2,0:T(8,128)(2,1)}, u32[]{:S(2)}, u32[]{:S(2)}) async-start(bf16[8,1152,144]{1,2,0:T(8,128)(2,1)} %stack.73), calls=%async_computation.1 | async-start | bytes 5308416 | tf_op jit(solution)/shard_map/all_to_all | solution.py:19
  211.5 109.7 %all-gather.12.cloned.1.call-start = ((), (), s32[]{:S(2)}) async-start(), calls=%async_computation.11 | async-start | bytes 1474560 | tf_op jit(solution)/shard_map/all_gather | solution.py:147
  230.2 146.4 %copy-start.40 = (f32[128]{0:T(128)}, f32[128]{0:T(128)S(1)}, u32[]{:S(2)}) copy-start(f32[128]{0:T(128)S(1)} %broadcast_multiply_fusion.4) | copy-start | bytes 1540
  230.4 146.2 %copy-start.44 = (f32[128]{0:T(128)}, f32[128]{0:T(128)S(1)}, u32[]{:S(2)}) copy-start(f32[128]{0:T(128)S(1)} %add_rsqrt_fusion) | copy-start | bytes 1540
  232.9 107.9 %all-gather.14.cloned.1.call-start = ((), (), s32[]{:S(2)}) async-start(), calls=%async_computation.13 | async-start | bytes 1474560 | tf_op jit(solution)/shard_map/all_gather | solution.py:155
  233.7 142.9 %reduce-scatter.16.cloned.1.call-start = ((), (), s32[]{:S(2)}) async-start(), calls=%async_computation.14 | async-start | bytes 1474560 | tf_op jit(solution)/shard_map/reduce_scatter | solution.py:158
  350.9 54.0 %reduce-scatter.14.cloned.1.call-start = ((), (), s32[]{:S(2)}) async-start(), calls=%async_computation.12 | async-start | bytes 1474560 | tf_op jit(solution)/shard_map/reduce_scatter | solution.py:150
  356.6 68.5 %all-gather.16.cloned.1.call-start = ((), (), s32[]{:S(2)}) async-start(), calls=%async_computation.15 | async-start | bytes 1474560 | tf_op jit(solution)/shard_map/all_gather | solution.py:155
  407.6 92.5 %reduce-scatter.22.cloned.1.call-start = ((), (), s32[]{:S(2)}) async-start(), calls=%async_computation.18 | async-start | bytes 2985984 | tf_op jit(solution)/shard_map/reduce_scatter | solution.py:367
  412.6 161.8 %reduce-scatter.24.cloned.1.call-start = ((), (), s32[]{:S(2)}) async-start(), calls=%async_computation.19 | async-start | bytes 2985984 | tf_op jit(solution)/shard_map/reduce_scatter | solution.py:370
  418.1 221.5 %reduce-scatter.20.cloned.1.call-start = ((), (), s32[]{:S(2)}) async-start(), calls=%async_computation.17 | async-start | bytes 995328 | tf_op jit(solution)/shard_map/reduce_scatter | solution.py:364
  438.9 227.5 %reduce-scatter.18.cloned.1.call-start = ((), (), s32[]{:S(2)}) async-start(), calls=%async_computation.16 | async-start | bytes 1474560 | tf_op jit(solution)/shard_map/reduce_scatter | solution.py:158
  452.3 328.0 %reduce-scatter.26.cloned.1.call-start = ((), (), s32[]{:S(2)}) async-start(), calls=%async_computation.22 | async-start | bytes 2322432
  474.4 196.0 %copy-start.17 = (bf16[128,1152]{1,0:T(8,128)(2,1)S(1)}, bf16[128,1152]{1,0:T(8,128)(2,1)}, u32[]{:S(2)}) copy-start(bf16[128,1152]{1,0:T(8,128)(2,1)} %reduce-scatter.12.cloned.1.call-done) | copy-start | bytes 884740
  474.4 197.7 %copy-start.10 = (bf16[128,1152]{1,0:T(8,128)(2,1)S(1)}, bf16[128,1152]{1,0:T(8,128)(2,1)}, u32[]{:S(2)}) copy-start(bf16[128,1152]{1,0:T(8,128)(2,1)} %reduce-scatter.16.cloned.1.call-done) | copy-start | bytes 884740
  474.6 166.5 %copy-start.33 = (f32[1,2,1152]{2,1,0:T(2,128)}, f32[1,2,1152]{2,1,0:T(2,128)S(1)}, u32[]{:S(2)}) copy-start(f32[1,2,1152]{2,1,0:T(2,128)S(1)} %dynamic_update_slice.8) | copy-start | bytes 27652
  501.9 173.4 %copy-start.18 = (bf16[128,1152]{1,0:T(8,128)(2,1)S(1)}, bf16[128,1152]{1,0:T(8,128)(2,1)}, u32[]{:S(2)}) copy-start(bf16[128,1152]{1,0:T(8,128)(2,1)} %reduce-scatter.14.cloned.1.call-done) | copy-start | bytes 884740
  (45 other events, 1105.5 us)
Sparse Core Ops, SparseCore 0:
  12.7 72.4 all-reduce.3
  115.8 16.3 all-gather.9
  134.5 55.3 all-gather.17
  204.7 24.1 reduce-scatter.11
  230.9 71.9 all-gather.19
  304.9 16.2 all-gather.11
  323.3 17.4 all-gather.13
  351.0 25.5 reduce-scatter.15
  379.2 25.6 reduce-scatter.13
  407.7 17.4 all-gather.15
  428.8 71.2 reduce-scatter.21
  503.6 70.7 reduce-scatter.23
  578.4 61.1 reduce-scatter.19
  642.0 24.3 reduce-scatter.17
  669.8 68.2 reduce-scatter.25
